TPU v7x, 32 devices: a whole 2x2x4 slice. The times are simulated.
32 devices in a mesh: dp: 4 (over y, x), expert: 8 (over z, core).
Axes of the slice: x: 2, y: 2, z: 4, core: 2. Of those that a mesh axis runs over, the one named last changes fastest.
Arguments:
- layer_input: bfloat16 [16384, 1280], P(('dp', 'expert')), may hold values from -6 to 6
- lengths: int32 [32], P(('dp', 'expert')), may hold values from 256 to 512, as said below
- expert_ids: int32 [16384, 7], P(('dp', 'expert')), may hold values from 0 to 14, all different within a row; in each aligned block of 512 rows (0 to 511, 512 to 1023, ...) at most 240 rows name the same one
- norm1: float32 [1280], replicated, may hold values from 0.5 to 1.5
- w_qkv: bfloat16 [1280, 3840], replicated, may hold values from -0.15625 to 0.15625
- w_out: bfloat16 [1280, 1280], replicated, may hold values from -1.25 to 1.25
- norm2: float32 [1280], replicated, may hold values from 0.5 to 1.5
- w_router: bfloat16 [1280, 16], replicated, may hold values from -0.078125 to 0.078125
- w_shared_in: bfloat16 [1280, 1792], replicated, may hold values from -0.15625 to 0.15625
- w_shared_down: bfloat16 [896, 1280], replicated, may hold values from -0.1875 to 0.1875
- w_expert_in: bfloat16 [16, 1280, 1792], P('expert'), may hold values from -0.15625 to 0.15625
- w_expert_down: bfloat16 [16, 896, 1280], P('expert'), may hold values from -1.5 to 1.5
- dout: bfloat16 [16384, 1280], P(('dp', 'expert')), may hold values from -6 to 6
Outputs:
- out: bfloat16 [16384, 1280], P(('dp', 'expert'))
- grad_x: float32 [16384, 1280], P(('dp', 'expert'))
- grad_norm1: float32 [1280], P(('dp', 'expert'))
- grad_qkv: float32 [1280, 3840], P(('dp', 'expert'))
- grad_out: float32 [1280, 1280], P(('dp', 'expert'))
- grad_norm2: float32 [1280], P(('dp', 'expert'))
- grad_router: float32 [1280, 16], P(('dp', 'expert'))
- grad_shared_in: float32 [1280, 1792], P(('dp', 'expert'))
- grad_shared_down: float32 [896, 1280], P(None, ('dp', 'expert'))
- grad_expert_in: float32 [16, 1280, 1792], P('expert', 'dp')
- grad_expert_down: float32 [16, 896, 1280], P('expert', 'dp')
- counts: int32 [16], replicated
Inputs may be any that keep to these rules, and one draw needn't show every extreme that they name: `expert_ids`: each row names 7 different routed experts. Among the rows of one sequence no expert is named more than 240 times, a bound that some block reaches. `lengths`: some sequence has exactly 512 live tokens and some exactly half of 512.
All inputs are finite; a program needn't handle non-finite values.
Results may differ from a plain program's by a relative error of at most 0.015.
Values may be sent and summed in bfloat16 or wider, within the bound.
No kernel may reach another device: no remote copies, remote signals or barrier semaphores. Data moves between devices by JAX's collectives and lax.ppermute only.
A program may use at most 384 MiB of HBM per device.

v0:
```python
import jax
import jax.numpy as jnp
from jax import lax
from jax.sharding import PartitionSpec as P

HEAD_DIM = 128
NORM_EPS = 1e-06
MASK_VALUE = -1e30
QUERY_BLOCK = 512


def silu_parts(gate_in):
    sigmoid_v = jax.nn.sigmoid(gate_in)
    return (gate_in * sigmoid_v, sigmoid_v * (1.0 + gate_in * (1.0 - sigmoid_v)))


def normalize(values_in, gain_vec):
    inverse = lax.rsqrt(jnp.mean(values_in * values_in, axis=-1, keepdims=True) + NORM_EPS)
    return (values_in * inverse * gain_vec, inverse)


def norm_back(incoming, values_in, inverse, gain_vec):
    scaled = values_in * inverse
    grad_gain = jnp.sum(incoming * scaled, axis=0)
    inner_grad = incoming * gain_vec
    grad_values = inverse * (
        inner_grad - scaled * jnp.mean(inner_grad * scaled, axis=-1, keepdims=True)
    )
    return (grad_values, grad_gain)


def rope_tables(seq_slots, head_width):
    half_dim = head_width // 2
    inv_freq = 1.0 / 10000.0 ** (jnp.arange(half_dim, dtype=jnp.float32) * 2.0 / head_width)
    angles = jnp.arange(seq_slots, dtype=jnp.float32)[:, None] * inv_freq[None, :]
    return (jnp.cos(angles)[:, None, :], jnp.sin(angles)[:, None, :])


def rotate(values_in, cosine, sine_t):
    half_dim = values_in.shape[-1] // 2
    first_half = values_in[..., :half_dim]
    second_half = values_in[..., half_dim:]
    return jnp.concatenate(
        [first_half * cosine - second_half * sine_t, first_half * sine_t + second_half * cosine],
        axis=-1,
    )


def score_block(query_block, keys_in, block_start, seq_length, score_scale):
    raw_scores = (
        jnp.einsum("qhd,khd->hqk", query_block, keys_in, preferred_element_type=jnp.float32)
        * score_scale
    )
    query_pos = block_start + jnp.arange(query_block.shape[0], dtype=jnp.int32)[:, None]
    key_pos = jnp.arange(keys_in.shape[0], dtype=jnp.int32)[None, :]
    allowed = (key_pos <= query_pos) & (key_pos < seq_length)
    return jnp.where(allowed[None], raw_scores, MASK_VALUE)


def attention_forward(queries, keys_in, values_in, seq_length):
    seq_slots, heads, head_width = queries.shape
    block_rows = min(QUERY_BLOCK, seq_slots)
    score_scale = head_width ** (-0.5)

    def one_block(block_index):
        block_start = block_index * block_rows
        scores = score_block(queries, keys_in, block_start, seq_length, score_scale)
        highest = jnp.max(scores, axis=-1, keepdims=True)
        weights_exp = jnp.exp(scores - highest)
        totals = jnp.sum(weights_exp, axis=-1, keepdims=True)
        probs_low = (weights_exp / totals).astype(jnp.bfloat16)
        block_out = jnp.einsum(
            "hqk,khd->qhd", probs_low, values_in, preferred_element_type=jnp.float32
        )
        return (block_out, highest + jnp.log(totals))

    block_outs, log_norm = lax.map(one_block, jnp.arange(seq_slots // block_rows))
    return (block_outs.reshape(seq_slots, heads, head_width), log_norm)


def attention_backward(queries, keys_in, values_in, grad_attended, log_norm, seq_length):
    seq_slots, heads, head_width = queries.shape
    block_rows = min(QUERY_BLOCK, seq_slots)
    score_scale = head_width ** (-0.5)

    def one_step(carried, block_in):
        grad_keys, grad_values = carried
        block_index, block_norm = block_in
        block_start = block_index * block_rows
        scores = score_block(queries, keys_in, block_start, seq_length, score_scale)
        probs = jnp.exp(scores - block_norm)
        grad_probs = jnp.einsum(
            "qhd,khd->hqk", grad_attended, values_in, preferred_element_type=jnp.float32
        )
        row_dot = jnp.sum(grad_probs * probs, axis=-1, keepdims=True)
        grad_scores = (probs * (grad_probs - row_dot)).astype(jnp.bfloat16)
        grad_query = (
            jnp.einsum("hqk,khd->qhd", grad_scores, keys_in, preferred_element_type=jnp.float32)
            * score_scale
        )
        grad_keys = (
            grad_keys
            + jnp.einsum("hqk,qhd->khd", grad_scores, queries, preferred_element_type=jnp.float32)
            * score_scale
        )
        grad_values = grad_values + jnp.einsum(
            "hqk,qhd->khd",
            probs.astype(jnp.bfloat16),
            grad_attended,
            preferred_element_type=jnp.float32,
        )
        return ((grad_keys, grad_values), grad_query)

    zeros_kv = jnp.zeros((seq_slots, heads, head_width), jnp.float32)
    (grad_keys, grad_values), grad_queries = lax.scan(
        one_step, (zeros_kv, zeros_kv), (jnp.arange(seq_slots // block_rows), log_norm)
    )
    return (grad_queries.reshape(seq_slots, heads, head_width), grad_keys, grad_values)


def reduce_experts(grad_in_part, grad_down_part):
    return (
        lax.psum_scatter(
            grad_in_part.astype(jnp.bfloat16), "dp", scatter_dimension=1, tiled=True
        ).astype(jnp.float32),
        lax.psum_scatter(
            grad_down_part.astype(jnp.bfloat16), "dp", scatter_dimension=1, tiled=True
        ).astype(jnp.float32),
    )


def per_device(
    layer_input,
    lengths,
    expert_ids,
    norm1,
    w_qkv,
    w_out,
    norm2,
    w_router,
    w_shared_in,
    w_shared_down,
    w_expert_in,
    w_expert_down,
    dout,
):
    seq_slots, width = layer_input.shape
    top_k = expert_ids.shape[1]
    experts = w_router.shape[1]
    local_experts = w_expert_in.shape[0]
    hidden_units = w_shared_down.shape[0]
    heads = width // HEAD_DIM
    capacity = (seq_slots * top_k // (experts - 1) // 8 + 1) * 8
    seq_length = lengths[0]
    live_rows = jnp.arange(seq_slots, dtype=jnp.int32) < seq_length
    live_col = live_rows.astype(jnp.float32)[:, None]
    cosine, sine_t = rope_tables(seq_slots, HEAD_DIM)
    x_full = layer_input.astype(jnp.float32)
    h1_full, inverse_one = normalize(x_full, norm1)
    h1_low = h1_full.astype(jnp.bfloat16)
    proj_qkv = jnp.dot(h1_low, w_qkv, preferred_element_type=jnp.float32).reshape(
        seq_slots, 3, heads, HEAD_DIM
    )
    queries = rotate(proj_qkv[:, 0], cosine, sine_t).astype(jnp.bfloat16)
    keys_in = rotate(proj_qkv[:, 1], cosine, sine_t).astype(jnp.bfloat16)
    values_in = proj_qkv[:, 2].astype(jnp.bfloat16)
    attended, log_norm = attention_forward(queries, keys_in, values_in, seq_length)
    attended_low = attended.reshape(seq_slots, width).astype(jnp.bfloat16)
    branch = jnp.dot(attended_low, w_out, preferred_element_type=jnp.float32)
    x_mid = x_full + live_col * branch
    h2_full, inverse_two = normalize(x_mid, norm2)
    h2_low = h2_full.astype(jnp.bfloat16)
    logits = jnp.dot(h2_low, w_router, preferred_element_type=jnp.float32)
    router_cols = jnp.arange(experts, dtype=jnp.int32) < experts - 1
    logits = jnp.where(router_cols[None, :], logits, MASK_VALUE)
    highest = jnp.max(logits, axis=-1, keepdims=True)
    weights_exp = jnp.exp(logits - highest)
    router_probs = weights_exp / jnp.sum(weights_exp, axis=-1, keepdims=True)
    choose_table = (
        expert_ids[:, :, None] == jnp.arange(experts, dtype=jnp.int32)[None, None, :]
    ).astype(jnp.float32)
    gates = jnp.sum(choose_table * router_probs[:, None, :], axis=-1)
    shared_gu = jnp.dot(h2_low, w_shared_in, preferred_element_type=jnp.float32)
    shared_act, shared_slope = silu_parts(shared_gu[:, :hidden_units])
    shared_up = shared_gu[:, hidden_units:]
    shared_hidden = (shared_act * shared_up).astype(jnp.bfloat16)
    shared_out = jnp.dot(shared_hidden, w_shared_down, preferred_element_type=jnp.float32)
    flat_ids = expert_ids.reshape(-1)
    live_flat = jnp.repeat(live_rows, top_k)
    pick_table = (
        (flat_ids[:, None] == jnp.arange(experts, dtype=jnp.int32)[None, :]) & live_flat[:, None]
    ).astype(jnp.int32)
    slot_rank = jnp.sum((jnp.cumsum(pick_table, axis=0) - pick_table) * pick_table, axis=-1)
    slot_index = jnp.where(live_flat, flat_ids * capacity + slot_rank, experts * capacity)
    slot_source = (
        jnp.full((experts * capacity,), seq_slots * top_k, jnp.int32)
        .at[slot_index]
        .set(jnp.arange(seq_slots * top_k, dtype=jnp.int32), mode="drop")
    )
    send_rows = jnp.take(h2_low, slot_source // top_k, axis=0, mode="fill", fill_value=0).reshape(
        experts, capacity, width
    )
    counts = lax.psum(jnp.sum(pick_table, axis=0), ("dp", "expert"))
    slot_rows = lax.all_to_all(send_rows, "expert", split_axis=0, concat_axis=0, tiled=True)
    slot_count = slot_rows.shape[1]
    grouped = slot_rows.reshape(-1, local_experts, slot_count, width)
    gate_up = jnp.einsum("nscd,sdf->nscf", grouped, w_expert_in, preferred_element_type=jnp.float32)
    activation, unused_slope = silu_parts(gate_up[..., :hidden_units])
    hidden_low = (activation * gate_up[..., hidden_units:]).astype(jnp.bfloat16)
    result_rows = jnp.einsum(
        "nscf,sfd->nscd", hidden_low, w_expert_down, preferred_element_type=jnp.float32
    ).astype(jnp.bfloat16)
    returned_rows = lax.all_to_all(
        result_rows.reshape(-1, slot_count, width),
        "expert",
        split_axis=0,
        concat_axis=0,
        tiled=True,
    )
    kept_gate_up = gate_up.reshape(-1, slot_count, 2 * hidden_units)
    picked = jnp.take(
        returned_rows.reshape(-1, width), slot_index, axis=0, mode="fill", fill_value=0
    ).reshape(seq_slots, top_k, width)
    picked_full = picked.astype(jnp.float32)
    routed_out = jnp.sum(gates[:, :, None] * picked_full, axis=1)
    result = (x_mid + live_col * (shared_out + routed_out)).astype(jnp.bfloat16)
    grad_top = dout.astype(jnp.float32)
    grad_branch = live_col * grad_top
    grad_branch_low = grad_branch.astype(jnp.bfloat16)
    grad_shared_down = jnp.dot(shared_hidden.T, grad_branch_low, preferred_element_type=jnp.float32)
    grad_hidden = jnp.dot(grad_branch_low, w_shared_down.T, preferred_element_type=jnp.float32)
    grad_shared_gu = jnp.concatenate(
        [grad_hidden * shared_up * shared_slope, grad_hidden * shared_act], axis=-1
    ).astype(jnp.bfloat16)
    grad_shared_in = jnp.dot(h2_low.T, grad_shared_gu, preferred_element_type=jnp.float32)
    grad_h2 = jnp.dot(grad_shared_gu, w_shared_in.T, preferred_element_type=jnp.float32)
    grad_picked = (
        (gates[:, :, None] * grad_branch[:, None, :]).astype(jnp.bfloat16).reshape(-1, width)
    )
    grad_gates = jnp.sum(picked_full * grad_branch[:, None, :], axis=-1)
    grad_send = jnp.take(grad_picked, slot_source, axis=0, mode="fill", fill_value=0).reshape(
        experts, capacity, width
    )
    grad_recv = lax.all_to_all(grad_send, "expert", split_axis=0, concat_axis=0, tiled=True)
    owners = grad_recv.shape[0] // local_experts
    grad_result = grad_recv.reshape(owners, local_experts, capacity, width)
    rows_held = slot_rows.reshape(owners, local_experts, capacity, width)
    gate_up_held = kept_gate_up.reshape(owners, local_experts, capacity, 2 * hidden_units)
    expert_act, expert_slope = silu_parts(gate_up_held[..., :hidden_units])
    expert_up = gate_up_held[..., hidden_units:]
    expert_hidden = (expert_act * expert_up).astype(jnp.bfloat16)
    grad_expert_down = jnp.einsum(
        "nscf,nscd->sfd", expert_hidden, grad_result, preferred_element_type=jnp.float32
    )
    grad_expert_hidden = jnp.einsum(
        "nscd,sfd->nscf", grad_result, w_expert_down, preferred_element_type=jnp.float32
    )
    grad_expert_gu = jnp.concatenate(
        [grad_expert_hidden * expert_up * expert_slope, grad_expert_hidden * expert_act], axis=-1
    ).astype(jnp.bfloat16)
    grad_expert_in = jnp.einsum(
        "nscd,nscf->sdf", rows_held, grad_expert_gu, preferred_element_type=jnp.float32
    )
    grad_rows = jnp.einsum(
        "nscf,sdf->nscd", grad_expert_gu, w_expert_in, preferred_element_type=jnp.float32
    ).astype(jnp.bfloat16)
    grad_back = lax.all_to_all(
        grad_rows.reshape(-1, capacity, width), "expert", split_axis=0, concat_axis=0, tiled=True
    )
    grad_slots = jnp.take(
        grad_back.reshape(-1, width), slot_index, axis=0, mode="fill", fill_value=0
    ).reshape(seq_slots, top_k, width)
    grad_h2 = grad_h2 + jnp.sum(grad_slots.astype(jnp.float32), axis=1)
    grad_probs = jnp.sum(choose_table * grad_gates[:, :, None], axis=1)
    grad_logits = (
        router_probs * (grad_probs - jnp.sum(grad_probs * router_probs, axis=-1, keepdims=True))
    ).astype(jnp.bfloat16)
    grad_router = jnp.dot(h2_low.T, grad_logits, preferred_element_type=jnp.float32)
    grad_h2 = grad_h2 + jnp.dot(grad_logits, w_router.T, preferred_element_type=jnp.float32)
    grad_mid_norm, grad_norm2 = norm_back(grad_h2, x_mid, inverse_two, norm2)
    grad_mid = grad_top + grad_mid_norm
    grad_attn_branch = (live_col * grad_mid).astype(jnp.bfloat16)
    grad_out_weight = jnp.dot(attended_low.T, grad_attn_branch, preferred_element_type=jnp.float32)
    grad_attended = (
        jnp.dot(grad_attn_branch, w_out.T, preferred_element_type=jnp.float32)
        .astype(jnp.bfloat16)
        .reshape(seq_slots, heads, HEAD_DIM)
    )
    grad_queries, grad_keys, grad_values = attention_backward(
        queries, keys_in, values_in, grad_attended, log_norm, seq_length
    )
    grad_proj = (
        jnp.stack(
            [
                rotate(grad_queries, cosine, -sine_t),
                rotate(grad_keys, cosine, -sine_t),
                grad_values,
            ],
            axis=1,
        )
        .astype(jnp.bfloat16)
        .reshape(seq_slots, 3 * width)
    )
    grad_qkv_weight = jnp.dot(h1_low.T, grad_proj, preferred_element_type=jnp.float32)
    grad_h1 = jnp.dot(grad_proj, w_qkv.T, preferred_element_type=jnp.float32)
    grad_in_norm, grad_norm1 = norm_back(grad_h1, x_full, inverse_one, norm1)
    grad_input = grad_mid + grad_in_norm
    expert_in_sum, expert_down_sum = reduce_experts(grad_expert_in, grad_expert_down)
    norm1_sum, qkv_sum, out_sum, norm2_sum, router_sum, shared_in_sum, shared_down_sum = (
        lax.psum_scatter(grad_norm1, ("dp", "expert"), scatter_dimension=0, tiled=True),
        lax.psum_scatter(grad_qkv_weight, ("dp", "expert"), scatter_dimension=0, tiled=True),
        lax.psum_scatter(grad_out_weight, ("dp", "expert"), scatter_dimension=0, tiled=True),
        lax.psum_scatter(grad_norm2, ("dp", "expert"), scatter_dimension=0, tiled=True),
        lax.psum_scatter(grad_router, ("dp", "expert"), scatter_dimension=0, tiled=True),
        lax.psum_scatter(grad_shared_in, ("dp", "expert"), scatter_dimension=0, tiled=True),
        lax.psum_scatter(grad_shared_down, ("dp", "expert"), scatter_dimension=1, tiled=True),
    )
    return (
        result,
        grad_input,
        norm1_sum,
        qkv_sum,
        out_sum,
        norm2_sum,
        router_sum,
        shared_in_sum,
        shared_down_sum,
        expert_in_sum,
        expert_down_sum,
        counts,
    )


def solution(mesh):
    return jax.shard_map(
        per_device,
        mesh=mesh,
        in_specs=(
            P(("dp", "expert"), None),
            P(("dp", "expert")),
            P(("dp", "expert"), None),
            P(),
            P(),
            P(),
            P(),
            P(),
            P(),
            P(),
            P("expert", None, None),
            P("expert", None, None),
            P(("dp", "expert"), None),
        ),
        out_specs=(
            P(("dp", "expert"), None),
            P(("dp", "expert"), None),
            P(("dp", "expert")),
            P(("dp", "expert"), None),
            P(("dp", "expert"), None),
            P(("dp", "expert")),
            P(("dp", "expert"), None),
            P(("dp", "expert"), None),
            P(None, ("dp", "expert")),
            P("expert", "dp", None),
            P("expert", "dp", None),
            P(),
        ),
        check_vma=False,
    )
```

profile of v0, /device:TPU:0, one launch (start us, length us, event | category | flops | bytes accessed | tf_op | source)
XLA Modules:
  0.0 1830.2 jit_solution(8007353251317582185)
XLA Ops:
  22.1 8.3 reduce-window.6
  36.7 14.0 scatter_custom_fusion
  55.0 8.8 fusion.63
  74.9 5.5 subtract_convert_fusion.3
  97.6 21.9 %gather_fusion = bf16[3840,1280]{1,0:T(8,128)(2,1)} fusion(bf16[512,1280]{1,0:T(8,128)(2,1)} %multiply_convert_fusion.4, s32[4096]{0:T(1024)S(1)} %copy-done.57), kind=kCustom, calls=%fused_computation.2 | custom fusion | bytes 19676160 | tf_op jit(solution)/shard_map/jit(_take)/gather | solution.py:200
  119.5 7.0 broadcast_select_fusion.1
  126.5 221.4 %all_to_all.20 = bf16[16,240,1280]{2,1,0:T(8,128)(2,1)S(1)} all-to-all(bf16[16,240,1280]{2,1,0:T(8,128)(2,1)S(1)} %broadcast_select_fusion.1), channel_id=1, replica_groups=mesh['dp'=4,'expert'=8] {'expert'}, dimensions={0} | all-to-all | bytes 19660800 | tf_op jit(solution)/shard_map/all_to_all | solution.py:204
  347.9 21.4 %convolution_bitcast_fusion = f32[8,2,240,1792]{3,2,0,1:T(8,128)} fusion(bf16[8,2,240,1280]{3,2,1,0:T(8,128)(2,1)S(1)} %bitcast.127, bf16[2,1280,1792]{2,1,0:T(8,128)(2,1)S(1)} %bitcast.139), kind=kOutput, calls=%fused_computation.20 | convolution fusion | flops 17616076800 | bytes 46530560 | tf_op jit(solution)/shard_map/nscd,sdf->nscf/dot_general | solution.py:207
  369.3 10.1 multiply_convert_fusion.1
  382.2 14.8 fusion.16
  397.0 8.1 copy.105
  405.1 5.4 all-to-all-start.1
  412.7 7.5 mul.573
  420.3 19.5 %mul.574 = f32[3584,1280]{1,0:T(8,128)} reshape(f32[512,7,1280]{2,1,0:T(8,128)} %mul.573) | data formatting | bytes 36700160 | tf_op jit(solution)/shard_map/mul | solution.py:238
  443.5 181.8 %all-to-all-done.1 = bf16[16,240,1280]{2,1,0:T(8,128)(2,1)} async-done(((bf16[16,240,1280]{2,1,0:T(8,128)(2,1)}), bf16[16,240,1280]{2,1,0:T(8,128)(2,1)}, u32[]{:S(2)}, u32[]{:S(2)}) %all-to-all-start.1) | async-done | bytes 9830432 | tf_op jit(solution)/shard_map/all_to_all | solution.py:213
  625.3 24.2 %gather_fusion.2 = bf16[3584,1280]{1,0:T(8,128)(2,1)} fusion(bf16[3840,1280]{1,0:T(8,128)(2,1)} %bitcast.17, s32[4096]{0:T(1024)S(1)} %pad_clamp_fusion.1), kind=kCustom, calls=%fused_computation.clone | custom fusion | bytes 18364416 | tf_op jit(solution)/shard_map/jit(_take)/gather | solution.py:221
  649.5 10.8 multiply_reduce_fusion.1
  664.5 11.5 multiply_convert_fusion
  676.1 25.4 %gather_fusion.1 = bf16[3840,1280]{1,0:T(8,128)(2,1)} fusion(bf16[3584,1280]{1,0:T(8,128)(2,1)} %multiply_convert_fusion, s32[4096]{0:T(1024)} %pad_clamp_fusion), kind=kCustom, calls=%fused_computation.3 | custom fusion | bytes 19676160 | tf_op jit(solution)/shard_map/jit(_take)/gather | solution.py:241
  701.4 9.6 broadcast_select_fusion
  711.0 5.2 all-to-all-start.2
  719.3 214.3 %all-to-all-done.2 = bf16[16,240,1280]{2,1,0:T(8,128)(2,1)} async-done(((bf16[16,240,1280]{2,1,0:T(8,128)(2,1)}), bf16[16,240,1280]{2,1,0:T(8,128)(2,1)}, u32[]{:S(2)}, u32[]{:S(2)}) %all-to-all-start.2) | async-done | bytes 9830432 | tf_op jit(solution)/shard_map/all_to_all | solution.py:244
  933.6 15.0 bitcast_convert_fusion.1
  948.7 26.2 %fusion.1 = (bf16[8,2,240,896]{3,2,0,1:T(8,128)(2,1)}, bf16[8,2,240,896]{3,2,0,1:T(8,128)(2,1)}) fusion(f32[8,2,240,1792]{3,2,0,1:T(8,128)} %convolution_bitcast_fusion, bf16[2,896,1280]{2,1,0:T(8,128)(2,1)} %param.26, bf16[8,2,240,1280]{3,2,1,0:T(8,128)(2,1)} %bitcast.19), kind=kOutput, calls=%fused_computation.13 | convolution fusion | flops 8852766720 | bytes 55705600 | tf_op jit(solution)/shard_map/nscd,sfd->nscf/dot_general | solution.py:255
  974.9 25.2 %bitcast_convert_fusion = bf16[2,1280,1792]{2,1,0:T(8,128)(2,1)} fusion(bf16[8,2,240,1280]{3,2,1,0:T(8,128)(2,1)} %bitcast.128, bf16[8,2,240,896]{3,2,0,1:T(8,128)(2,1)} %get-tuple-element.79, bf16[8,2,240,896]{3,2,0,1:T(8,128)(2,1)} %get-tuple-element.78), kind=kOutput, calls=%fused_computation.6 | convolution fusion | flops 17648189440 | bytes 32768000 | tf_op jit(solution)/shard_map/nscd,nscf->sdf/dot_general | solution.py:261
  1000.7 5.4 fusion.89
  1014.4 25.1 %fusion.17 = bf16[8,2,240,1280]{3,2,0,1:T(8,128)(2,1)} fusion(bf16[2,1280,1792]{2,1,0:T(8,128)(2,1)} %param.25, bf16[8,2,240,896]{3,2,0,1:T(8,128)(2,1)} %get-tuple-element.79, bf16[8,2,240,896]{3,2,0,1:T(8,128)(2,1)} %get-tuple-element.78), kind=kOutput, calls=%fused_computation.43 | convolution fusion | flops 17648517120 | bytes 32768000 | tf_op jit(solution)/shard_map/nscf,sdf->nscd/dot_general | solution.py:264
  1039.6 8.5 copy.108
  1048.0 5.2 all-to-all-start.3
  1053.3 8.3 fusion.52
  1061.8 260.5 %all-to-all-done.3 = bf16[16,240,1280]{2,1,0:T(8,128)(2,1)} async-done(((bf16[16,240,1280]{2,1,0:T(8,128)(2,1)}), bf16[16,240,1280]{2,1,0:T(8,128)(2,1)}, u32[]{:S(2)}, u32[]{:S(2)}) %all-to-all-start.3) | async-done | bytes 9830432 | tf_op jit(solution)/shard_map/all_to_all | solution.py:267
  1322.3 24.3 %gather_fusion.3 = bf16[3584,1280]{1,0:T(8,128)(2,1)} fusion(bf16[3840,1280]{1,0:T(8,128)(2,1)} %bitcast.25, s32[4096]{0:T(1024)S(1)} %copy-done.52), kind=kCustom, calls=%fused_computation.1.clone | custom fusion | bytes 18364416 | tf_op jit(solution)/shard_map/jit(_take)/gather | solution.py:270
  1346.6 18.9 %select_convert_fusion = (f32[3584,1280]{1,0:T(8,128)}, f32[3584,1280]{1,0:T(8,128)}) fusion(bf16[3584,1280]{1,0:T(8,128)(2,1)} %gather_fusion.3, pred[3584]{0:T(1024)(128)(4,1)S(1)} %copy-done.61, bf16[3584,1280]{1,0:T(8,128)(2,1)} %gather_fusion.2), kind=kLoop, calls=%fused_computation.36 | loop fusion | flops 18350080 | bytes 55053824 | tf_op jit(solution)/shard_map/convert_element_type | solution.py:273
  1365.4 19.3 %reshape.325 = f32[512,7,1280]{2,1,0:T(8,128)} reshape(f32[3584,1280]{1,0:T(8,128)} %get-tuple-element.98) | data formatting | bytes 36700160 | tf_op jit(solution)/shard_map/convert_element_type | solution.py:273
  1384.7 12.3 reduce_sum.165
  1397.0 6.4 convolution_add_fusion.2
  1407.0 4.7 fusion.85
  1412.5 4.7 convolution_convert_fusion.2
  1419.9 11.3 multiply_reduce_fusion.2
  1431.2 6.3 multiply_convert_fusion.2
  1449.0 6.3 copy.121
  1455.3 12.5 fusion.61
  1468.5 38.3 %psum.7 = s32[16]{0:T(128)} all-reduce(s32[16]{0:T(128)S(1)} %copy-done.74), channel_id=1, replica_groups=mesh['dp'=4,'expert'=8] {'dp','expert'}, use_global_device_ids=true, to_apply=%region_31.33 | all-reduce | flops 16 | bytes 128 | tf_op jit(solution)/shard_map/psum | solution.py:203
  1511.0 12.1 fusion.41
  1523.1 42.4 %all-reduce.4 = (f32[1280]{0:T(1024)S(1)}, f32[1280]{0:T(1024)S(1)}) all-reduce(f32[1280]{0:T(1024)S(1)} %get-tuple-element.56, f32[1280]{0:T(1024)S(1)} %get-tuple-element.54), channel_id=2, replica_groups=mesh['dp'=4,'expert'=8] {'dp','expert'}, use_global_device_ids=true, to_apply=%region_20.22.clone | all-reduce | flops 2560 | bytes 20480
  1566.7 19.3 %reshape.324 = f32[512,7,1280]{2,1,0:T(8,128)} reshape(f32[3584,1280]{1,0:T(8,128)} %get-tuple-element.99) | data formatting | bytes 36700160 | tf_op jit(solution)/shard_map/convert_element_type | solution.py:224
  1586.6 28.3 %multiply_reduce_fusion = f32[512,1280]{1,0:T(8,128)S(1)} fusion(f32[512,7,1280]{2,1,0:T(8,128)} %reshape.324, f32[512,7]{1,0:T(8,128)S(1)} %copy-done.28), kind=kLoop, calls=%fused_computation.5 | loop fusion | flops 8519680 | bytes 20985856 | tf_op jit(solution)/shard_map/reduce_sum | solution.py:225
  1625.2 197.3 %reduce-scatter.11.cloned.1.call-done = f32[40,3840]{1,0:T(8,128)} async-done(((f32[1280,3840]{1,0:T(8,128)}), f32[40,3840]{1,0:T(8,128)}) %reduce-scatter.11.cloned.1.call-update) | async-done | bytes 614416 | tf_op jit(solution)/shard_map/reduce_scatter | solution.py:311
  (263 shorter events, 112.4 us)
Async XLA Ops:
  8.0 84.4 %copy-start = (bf16[1280,1280]{1,0:T(8,128)(2,1)S(1)}, bf16[1280,1280]{1,0:T(8,128)(2,1)}, u32[]{:S(2)}) copy-start(bf16[1280,1280]{1,0:T(8,128)(2,1)} %param.20) | copy-start | bytes 9830404
  15.3 48.4 %copy-start.44 = (s32[3584]{0:T(1024)}, s32[3584]{0:T(1024)S(1)}, u32[]{:S(2)}) copy-start(s32[3584]{0:T(1024)S(1)} %eq.41) | copy-start | bytes 43012
  55.0 20.0 %copy-start.25 = (f32[512,64]{1,0:T(8,128)}, f32[512,64]{1,0:T(8,128)S(1)}, u32[]{:S(2)}) copy-start(f32[512,64]{1,0:T(8,128)S(1)} %get-tuple-element.102) | copy-start | bytes 393220
  97.6 21.9 %copy-start.71 = (pred[16,240]{1,0:T(8,128)(4,1)S(1)}, pred[16,240]{1,0:T(8,128)(4,1)}, u32[]{:S(2)}) copy-start(pred[16,240]{1,0:T(8,128)(4,1)} %broadcast_in_dim.145) | copy-start | bytes 11524
  119.5 228.4 %slice-start.3 = ((s8[9175040]{0:T(1024)(128)(4,1)}), s8[4194304]{0:T(1024)(128)(4,1)S(1)}, s32[]{:S(2)}) async-start(s8[9175040]{0:T(1024)(128)(4,1)} %bitcast.138), calls=%async_computation.20 | async-start | bytes 8388608
  119.5 228.4 %slice-start.4 = ((s8[9175040]{0:T(1024)(128)(4,1)}), s8[4194304]{0:T(1024)(128)(4,1)S(1)}, s32[]{:S(2)}) async-start(s8[9175040]{0:T(1024)(128)(4,1)} %bitcast.138), calls=%async_computation.21 | async-start | bytes 8388608
  126.5 221.4 %slice-start.5 = ((s8[9175040]{0:T(1024)(128)(4,1)}), s8[786432]{0:T(1024)(128)(4,1)S(1)}, s32[]{:S(2)}) async-start(s8[9175040]{0:T(1024)(128)(4,1)} %bitcast.138), calls=%async_computation.22 | async-start | bytes 1572864
  347.9 21.4 %copy-start.18 = (bf16[16,240,1280]{2,1,0:T(8,128)(2,1)}, bf16[16,240,1280]{2,1,0:T(8,128)(2,1)S(1)}, u32[]{:S(2)}) copy-start(bf16[16,240,1280]{2,1,0:T(8,128)(2,1)S(1)} %all_to_all.20) | copy-start | bytes 29491204
  405.1 220.2 %all-to-all-start.1 = ((bf16[16,240,1280]{2,1,0:T(8,128)(2,1)}), bf16[16,240,1280]{2,1,0:T(8,128)(2,1)}, u32[]{:S(2)}, u32[]{:S(2)}) async-start(bf16[16,240,1280]{2,1,0:T(8,128)(2,1)} %bitcast.119), calls=%async_computation.1 | async-start | bytes 19660800 | tf_op jit(solution)/shard_map/all_to_all | solution.py:213
  420.3 19.5 %copy-start.45 = (s32[3584]{0:T(1024)S(1)}, s32[3584]{0:T(1024)}, u32[]{:S(2)}) copy-start(s32[3584]{0:T(1024)} %copy-done.44) | copy-start | bytes 43012
  420.3 19.5 %copy-start.48 = (s32[3584]{0:T(1024)S(1)}, s32[3584]{0:T(1024)}, u32[]{:S(2)}) copy-start(s32[3584]{0:T(1024)} %copy-done.47) | copy-start | bytes 43012
  420.3 19.5 %copy-start.62 = (pred[3584]{0:T(1024)(128)(4,1)S(1)}, pred[3584]{0:T(1024)(128)(4,1)}, u32[]{:S(2)}) copy-start(pred[3584]{0:T(1024)(128)(4,1)} %and.62) | copy-start | bytes 10756
  420.3 19.5 %copy-start.50 = (s32[3840]{0:T(1024)S(1)}, s32[3840]{0:T(1024)}, u32[]{:S(2)}) copy-start(s32[3840]{0:T(1024)} %copy-done.49) | copy-start | bytes 46084
  420.3 20.2 %copy-start.40 = (bf16[1280,16]{0,1:T(8,128)(2,1)S(1)}, bf16[1280,16]{0,1:T(8,128)(2,1)}, u32[]{:S(2)}) copy-start(bf16[1280,16]{0,1:T(8,128)(2,1)} %param.22) | copy-start | bytes 122884
  439.8 209.7 %copy-start.60 = (pred[3584]{0:T(1024)(128)(4,1)}, pred[3584]{0:T(1024)(128)(4,1)S(1)}, u32[]{:S(2)}) copy-start(pred[3584]{0:T(1024)(128)(4,1)S(1)} %get-tuple-element.74) | copy-start | bytes 10756
  439.8 209.7 %copy-start.51 = (s32[4096]{0:T(1024)}, s32[4096]{0:T(1024)S(1)}, u32[]{:S(2)}) copy-start(s32[4096]{0:T(1024)S(1)} %pad_clamp_fusion.1) | copy-start | bytes 49156
  442.9 206.6 %copy-start.65 = (f32[512]{0:T(512)}, f32[512]{0:T(512)S(1)}, u32[]{:S(2)}) copy-start(f32[512]{0:T(512)S(1)} %fusion.74) | copy-start | bytes 6148
  649.5 12.5 copy-start.46
  664.3 11.8 copy-start.27
  676.1 25.4 %copy-start.70 = (pred[16,240]{1,0:T(8,128)(4,1)S(1)}, pred[16,240]{1,0:T(8,128)(4,1)}, u32[]{:S(2)}) copy-start(pred[16,240]{1,0:T(8,128)(4,1)} %broadcast_in_dim.150) | copy-start | bytes 11524
  711.0 222.6 %all-to-all-start.2 = ((bf16[16,240,1280]{2,1,0:T(8,128)(2,1)}), bf16[16,240,1280]{2,1,0:T(8,128)(2,1)}, u32[]{:S(2)}, u32[]{:S(2)}) async-start(bf16[16,240,1280]{2,1,0:T(8,128)(2,1)} %broadcast_select_fusion), calls=%async_computation.2 | async-start | bytes 19660800 | tf_op jit(solution)/shard_map/all_to_all | solution.py:244
  716.2 790.5 %all-reduce.7.cloned.1.call-start = ((), (), s32[]{:S(2)}) async-start(), calls=%async_computation.15 | async-start | bytes 163840
  719.3 788.9 %reduce-scatter.19.cloned.1.call-start = ((), (), s32[]{:S(2)}) async-start(), calls=%async_computation.14 | async-start | bytes 5734400 | tf_op jit(solution)/shard_map/reduce_scatter | solution.py:126
  948.7 672.2 %reduce-scatter.17.cloned.1.call-start = ((), (), s32[]{:S(2)}) async-start(), calls=%async_computation.13 | async-start | bytes 11468800 | tf_op jit(solution)/shard_map/reduce_scatter | solution.py:123
  1000.2 5.9 copy-start.64
  1000.2 625.0 %reduce-scatter.21.cloned.1.call-start = ((), (), s32[]{:S(2)}) async-start(), calls=%async_computation.16 | async-start | bytes 4730880
  1048.0 274.3 %all-to-all-start.3 = ((bf16[16,240,1280]{2,1,0:T(8,128)(2,1)}), bf16[16,240,1280]{2,1,0:T(8,128)(2,1)}, u32[]{:S(2)}, u32[]{:S(2)}) async-start(bf16[16,240,1280]{2,1,0:T(8,128)(2,1)} %bitcast.120), calls=%async_computation.3 | async-start | bytes 19660800 | tf_op jit(solution)/shard_map/all_to_all | solution.py:267
  1053.2 572.0 %reduce-scatter.15.cloned.1.call-start = ((), (), s32[]{:S(2)}) async-start(), calls=%async_computation.12 | async-start | bytes 9461760 | tf_op jit(solution)/shard_map/reduce_scatter | solution.py:315
  1061.6 260.7 %copy-start.52 = (s32[4096]{0:T(1024)S(1)}, s32[4096]{0:T(1024)}, u32[]{:S(2)}) copy-start(s32[4096]{0:T(1024)} %copy-done.51) | copy-start | bytes 49156
  1061.6 563.6 %reduce-scatter.13.cloned.1.call-start = ((), (), s32[]{:S(2)}) async-start(), calls=%async_computation.11 | async-start | bytes 6758400 | tf_op jit(solution)/shard_map/reduce_scatter | solution.py:312
  1322.3 24.3 %copy-start.61 = (pred[3584]{0:T(1024)(128)(4,1)S(1)}, pred[3584]{0:T(1024)(128)(4,1)}, u32[]{:S(2)}) copy-start(pred[3584]{0:T(1024)(128)(4,1)} %copy-done.60) | copy-start | bytes 10756
  1397.0 6.4 copy-start.3
  1397.0 6.4 copy-start.41
  1397.0 6.4 copy-start.43
  1397.0 6.4 copy-start.56
  1397.0 6.4 copy-start.68
  1411.8 410.8 %reduce-scatter.11.cloned.1.call-start = ((), (), s32[]{:S(2)}) async-start(), calls=%async_computation.10 | async-start | bytes 20275200 | tf_op jit(solution)/shard_map/reduce_scatter | solution.py:311
  1419.9 11.3 slice-start
  1419.9 11.3 slice-start.1
  1419.9 11.3 slice-start.2
  1431.2 6.4 copy-start.15
  1431.2 6.4 copy-start.17
  1449.0 6.3 copy-start.72
  1449.0 6.3 copy-start.73
  1566.7 20.0 %copy-start.28 = (f32[512,7]{1,0:T(8,128)S(1)}, f32[512,7]{1,0:T(8,128)}, u32[]{:S(2)}) copy-start(f32[512,7]{1,0:T(8,128)} %copy-done.27) | copy-start | bytes 43012
  1586.6 28.3 %copy-start.4 = (f32[512,1280]{1,0:T(8,128)S(1)}, f32[512,1280]{1,0:T(8,128)}, u32[]{:S(2)}) copy-start(f32[512,1280]{1,0:T(8,128)} %copy-done.2) | copy-start | bytes 7864324
  1586.6 28.3 %copy-start.32 = (bf16[512,896]{1,0:T(8,128)(2,1)S(1)}, bf16[512,896]{1,0:T(8,128)(2,1)}, u32[]{:S(2)}) copy-start(bf16[512,896]{1,0:T(8,128)(2,1)} %copy-done.31) | copy-start | bytes 2752516
  1586.6 28.3 %copy-start.76 = (bf16[896,1280]{1,0:T(8,128)(2,1)S(1)}, bf16[896,1280]{1,0:T(8,128)(2,1)}, u32[]{:S(2)}) copy-start(bf16[896,1280]{1,0:T(8,128)(2,1)} %param.24) | copy-start | bytes 6881284
  (45 other events, 131.2 us)
Sparse Core Ops, SparseCore 0:
  722.7 169.1 all-reduce.6
Sparse Core Ops, SparseCore 1:
  948.7 54.8 reduce-scatter.18
  1006.7 92.7 reduce-scatter.16
  1102.1 199.6 reduce-scatter.20
  1304.7 153.0 reduce-scatter.14
  1460.6 145.8 reduce-scatter.12
  1613.5 209.0 reduce-scatter.10
where the time goes:
time: 1840 us; the launch traced here: 1830 us
  waiting for transfers between devices  854 us (46%)
  blocking collectives  302 us (16%)
  local copies, waits for them, and re-layouts  239 us (13%)
  matrix products  233 us (13%)
  other arithmetic  167 us (9%)
    all_to_all x1, waiting for transfers between devices, per_device(): lax.all_to_all(grad_rows.reshape(-1, capacity, width), 'expert', split_ax...  260 us
    all_to_all x1, blocking collectives, per_device(): lax.all_to_all(send_rows, 'expert', split_axis=0, concat_axis=0, tiled=True)  221 us
    all_to_all x1, waiting for transfers between devices, per_device(): lax.all_to_all(grad_send, 'expert', split_axis=0, concat_axis=0, tiled=True)  214 us
    reduce_scatter x1, waiting for transfers between devices, per_device(): lax.psum_scatter(grad_qkv_weight, ('dp', 'expert'), scatter_dimension=0,...  197 us
    all_to_all x1, waiting for transfers between devices, per_device(): lax.all_to_all(result_rows.reshape(-1, slot_count, width), 'expert', spli...  182 us
    unnamed x1, blocking collectives  42.4 us
    psum x1, blocking collectives, per_device(): counts = lax.psum(jnp.sum(pick_table, axis=0), ('dp', 'expert'))  38.3 us
  transfers between devices with their start and end apart: 10, of which 4 were waited for; matrix products, arithmetic and copies ran while one was open for 20% of the time, Pallas kernels for 0%

commit v1 on v0

--- a/solution.py
+++ b/solution.py
@@ -200,7 +200,8 @@
     send_rows = jnp.take(h2_low, slot_source // top_k, axis=0, mode="fill", fill_value=0).reshape(
         experts, capacity, width
     )
-    counts = lax.psum(jnp.sum(pick_table, axis=0), ("dp", "expert"))
+    partial = lax.psum(jnp.sum(pick_table, axis=0), "expert")
+    counts = lax.psum(partial, "dp")
     slot_rows = lax.all_to_all(send_rows, "expert", split_axis=0, concat_axis=0, tiled=True)
     slot_count = slot_rows.shape[1]
     grouped = slot_rows.reshape(-1, local_experts, slot_count, width)

time: 1840 us -> 1840 us (level)
  waiting for transfers between devices: 854 us -> 881 us
  blocking collectives: 302 us -> 276 us
    psum x1 -> x2, blocking collectives: 38.3 us -> 13.8 us  [the longest x1 8.1 us: per_device(): counts = lax.psum(partial, 'dp')]
  transfers between devices with their start and end apart: 10 -> 10, of which waited for: 4 -> 5; matrix products, arithmetic and copies ran while one was open for 20% -> 20% of each run, Pallas kernels for 0% -> 0%
where the time goes in v1:
time: 1840 us; the launch traced here: 1830 us
  waiting for transfers between devices  881 us (48%)
  blocking collectives  276 us (15%)
  local copies, waits for them, and re-layouts  239 us (13%)
  matrix products  233 us (13%)
  other arithmetic  167 us (9%)
    all_to_all x1, waiting for transfers between devices, per_device(): lax.all_to_all(grad_rows.reshape(-1, capacity, width), 'expert', split_ax...  260 us
    all_to_all x1, blocking collectives, per_device(): lax.all_to_all(send_rows, 'expert', split_axis=0, concat_axis=0, tiled=True)  221 us
    reduce_scatter x1, waiting for transfers between devices, per_device(): lax.psum_scatter(grad_qkv_weight, ('dp', 'expert'), scatter_dimension=0,...  215 us
    all_to_all x1, waiting for transfers between devices, per_device(): lax.all_to_all(grad_send, 'expert', split_axis=0, concat_axis=0, tiled=True)  214 us
    all_to_all x1, waiting for transfers between devices, per_device(): lax.all_to_all(result_rows.reshape(-1, slot_count, width), 'expert', spli...  182 us
    unnamed x1, blocking collectives  40.4 us
  transfers between devices with their start and end apart: 10, of which 5 were waited for; matrix products, arithmetic and copies ran while one was open for 20% of the time, Pallas kernels for 0%

profile of v1, /device:TPU:0, one launch (start us, length us, event | category | flops | bytes accessed | tf_op | source)
XLA Modules:
  0.0 1830.7 jit_solution(4156918328064807847)
XLA Ops:
  22.1 8.3 reduce-window.6
  36.7 14.0 scatter_custom_fusion
  55.0 8.8 fusion.63
  74.9 5.4 subtract_convert_fusion.3
  97.5 21.9 %gather_fusion = bf16[3840,1280]{1,0:T(8,128)(2,1)} fusion(bf16[512,1280]{1,0:T(8,128)(2,1)} %multiply_convert_fusion.4, s32[4096]{0:T(1024)S(1)} %copy-done.57), kind=kCustom, calls=%fused_computation.2 | custom fusion | bytes 19676160 | tf_op jit(solution)/shard_map/jit(_take)/gather | solution.py:200
  119.5 7.0 broadcast_select_fusion.1
  126.5 221.4 %all_to_all.20 = bf16[16,240,1280]{2,1,0:T(8,128)(2,1)S(1)} all-to-all(bf16[16,240,1280]{2,1,0:T(8,128)(2,1)S(1)} %broadcast_select_fusion.1), channel_id=1, replica_groups=mesh['dp'=4,'expert'=8] {'expert'}, dimensions={0} | all-to-all | bytes 19660800 | tf_op jit(solution)/shard_map/all_to_all | solution.py:205
  347.9 21.4 %convolution_bitcast_fusion = f32[8,2,240,1792]{3,2,0,1:T(8,128)} fusion(bf16[8,2,240,1280]{3,2,1,0:T(8,128)(2,1)S(1)} %bitcast.127, bf16[2,1280,1792]{2,1,0:T(8,128)(2,1)S(1)} %bitcast.139), kind=kOutput, calls=%fused_computation.20 | convolution fusion | flops 17616076800 | bytes 46530560 | tf_op jit(solution)/shard_map/nscd,sdf->nscf/dot_general | solution.py:208
  369.3 10.1 multiply_convert_fusion.1
  382.1 14.8 fusion.16
  396.9 8.1 copy.105
  405.0 5.4 all-to-all-start.1
  412.6 7.5 mul.573
  420.2 19.4 %mul.574 = f32[3584,1280]{1,0:T(8,128)} reshape(f32[512,7,1280]{2,1,0:T(8,128)} %mul.573) | data formatting | bytes 36700160 | tf_op jit(solution)/shard_map/mul | solution.py:239
  443.4 181.8 %all-to-all-done.1 = bf16[16,240,1280]{2,1,0:T(8,128)(2,1)} async-done(((bf16[16,240,1280]{2,1,0:T(8,128)(2,1)}), bf16[16,240,1280]{2,1,0:T(8,128)(2,1)}, u32[]{:S(2)}, u32[]{:S(2)}) %all-to-all-start.1) | async-done | bytes 9830432 | tf_op jit(solution)/shard_map/all_to_all | solution.py:214
  625.2 24.2 %gather_fusion.2 = bf16[3584,1280]{1,0:T(8,128)(2,1)} fusion(bf16[3840,1280]{1,0:T(8,128)(2,1)} %bitcast.17, s32[4096]{0:T(1024)S(1)} %pad_clamp_fusion.1), kind=kCustom, calls=%fused_computation.clone | custom fusion | bytes 18364416 | tf_op jit(solution)/shard_map/jit(_take)/gather | solution.py:222
  649.4 10.8 multiply_reduce_fusion.1
  664.4 11.5 multiply_convert_fusion
  676.0 25.4 %gather_fusion.1 = bf16[3840,1280]{1,0:T(8,128)(2,1)} fusion(bf16[3584,1280]{1,0:T(8,128)(2,1)} %multiply_convert_fusion, s32[4096]{0:T(1024)} %pad_clamp_fusion), kind=kCustom, calls=%fused_computation.3 | custom fusion | bytes 19676160 | tf_op jit(solution)/shard_map/jit(_take)/gather | solution.py:242
  701.3 9.5 broadcast_select_fusion
  710.9 5.2 all-to-all-start.2
  719.2 214.3 %all-to-all-done.2 = bf16[16,240,1280]{2,1,0:T(8,128)(2,1)} async-done(((bf16[16,240,1280]{2,1,0:T(8,128)(2,1)}), bf16[16,240,1280]{2,1,0:T(8,128)(2,1)}, u32[]{:S(2)}, u32[]{:S(2)}) %all-to-all-start.2) | async-done | bytes 9830432 | tf_op jit(solution)/shard_map/all_to_all | solution.py:245
  933.5 15.0 bitcast_convert_fusion.1
  948.6 26.2 %fusion.1 = (bf16[8,2,240,896]{3,2,0,1:T(8,128)(2,1)}, bf16[8,2,240,896]{3,2,0,1:T(8,128)(2,1)}) fusion(f32[8,2,240,1792]{3,2,0,1:T(8,128)} %convolution_bitcast_fusion, bf16[2,896,1280]{2,1,0:T(8,128)(2,1)} %param.26, bf16[8,2,240,1280]{3,2,1,0:T(8,128)(2,1)} %bitcast.19), kind=kOutput, calls=%fused_computation.13 | convolution fusion | flops 8852766720 | bytes 55705600 | tf_op jit(solution)/shard_map/nscd,sfd->nscf/dot_general | solution.py:256
  974.8 25.2 %bitcast_convert_fusion = bf16[2,1280,1792]{2,1,0:T(8,128)(2,1)} fusion(bf16[8,2,240,1280]{3,2,1,0:T(8,128)(2,1)} %bitcast.128, bf16[8,2,240,896]{3,2,0,1:T(8,128)(2,1)} %get-tuple-element.79, bf16[8,2,240,896]{3,2,0,1:T(8,128)(2,1)} %get-tuple-element.78), kind=kOutput, calls=%fused_computation.6 | convolution fusion | flops 17648189440 | bytes 32768000 | tf_op jit(solution)/shard_map/nscd,nscf->sdf/dot_general | solution.py:262
  1000.6 5.4 fusion.89
  1014.3 25.2 %fusion.17 = bf16[8,2,240,1280]{3,2,0,1:T(8,128)(2,1)} fusion(bf16[2,1280,1792]{2,1,0:T(8,128)(2,1)} %param.25, bf16[8,2,240,896]{3,2,0,1:T(8,128)(2,1)} %get-tuple-element.79, bf16[8,2,240,896]{3,2,0,1:T(8,128)(2,1)} %get-tuple-element.78), kind=kOutput, calls=%fused_computation.43 | convolution fusion | flops 17648517120 | bytes 32768000 | tf_op jit(solution)/shard_map/nscf,sdf->nscd/dot_general | solution.py:265
  1039.5 8.4 copy.108
  1047.9 5.2 all-to-all-start.3
  1053.2 8.3 fusion.52
  1061.7 260.2 %all-to-all-done.3 = bf16[16,240,1280]{2,1,0:T(8,128)(2,1)} async-done(((bf16[16,240,1280]{2,1,0:T(8,128)(2,1)}), bf16[16,240,1280]{2,1,0:T(8,128)(2,1)}, u32[]{:S(2)}, u32[]{:S(2)}) %all-to-all-start.3) | async-done | bytes 9830432 | tf_op jit(solution)/shard_map/all_to_all | solution.py:268
  1321.9 24.2 %gather_fusion.3 = bf16[3584,1280]{1,0:T(8,128)(2,1)} fusion(bf16[3840,1280]{1,0:T(8,128)(2,1)} %bitcast.25, s32[4096]{0:T(1024)S(1)} %copy-done.52), kind=kCustom, calls=%fused_computation.1.clone | custom fusion | bytes 18364416 | tf_op jit(solution)/shard_map/jit(_take)/gather | solution.py:271
  1346.2 18.8 %select_convert_fusion = (f32[3584,1280]{1,0:T(8,128)}, f32[3584,1280]{1,0:T(8,128)}) fusion(bf16[3584,1280]{1,0:T(8,128)(2,1)} %gather_fusion.3, pred[3584]{0:T(1024)(128)(4,1)S(1)} %copy-done.61, bf16[3584,1280]{1,0:T(8,128)(2,1)} %gather_fusion.2), kind=kLoop, calls=%fused_computation.36 | loop fusion | flops 18350080 | bytes 55053824 | tf_op jit(solution)/shard_map/convert_element_type | solution.py:274
  1365.0 19.2 %reshape.325 = f32[512,7,1280]{2,1,0:T(8,128)} reshape(f32[3584,1280]{1,0:T(8,128)} %get-tuple-element.98) | data formatting | bytes 36700160 | tf_op jit(solution)/shard_map/convert_element_type | solution.py:274
  1384.3 12.3 reduce_sum.165
  1396.6 6.4 convolution_add_fusion.2
  1419.5 11.3 multiply_reduce_fusion.2
  1430.8 6.3 multiply_convert_fusion.2
  1448.7 6.3 copy.121
  1455.0 12.5 fusion.61
  1468.1 5.7 psum.14
  1473.9 8.1 psum.15
  1486.3 12.1 fusion.41
  1498.3 40.4 %all-reduce.4 = (f32[1280]{0:T(1024)S(1)}, f32[1280]{0:T(1024)S(1)}) all-reduce(f32[1280]{0:T(1024)S(1)} %get-tuple-element.56, f32[1280]{0:T(1024)S(1)} %get-tuple-element.54), channel_id=2, replica_groups=mesh['dp'=4,'expert'=8] {'dp','expert'}, use_global_device_ids=true, to_apply=%region_20.22.clone | all-reduce | flops 2560 | bytes 20480
  1539.9 19.3 %reshape.324 = f32[512,7,1280]{2,1,0:T(8,128)} reshape(f32[3584,1280]{1,0:T(8,128)} %get-tuple-element.99) | data formatting | bytes 36700160 | tf_op jit(solution)/shard_map/convert_element_type | solution.py:225
  1559.9 28.3 %multiply_reduce_fusion = f32[512,1280]{1,0:T(8,128)S(1)} fusion(f32[512,7,1280]{2,1,0:T(8,128)} %reshape.324, f32[512,7]{1,0:T(8,128)S(1)} %copy-done.28), kind=kLoop, calls=%fused_computation.5 | loop fusion | flops 8519680 | bytes 20985856 | tf_op jit(solution)/shard_map/reduce_sum | solution.py:226
  1598.0 9.7 reduce-scatter.13.cloned.1.call-done
  1607.7 215.3 %reduce-scatter.11.cloned.1.call-done = f32[40,3840]{1,0:T(8,128)} async-done(((f32[1280,3840]{1,0:T(8,128)}), f32[40,3840]{1,0:T(8,128)}) %reduce-scatter.11.cloned.1.call-update) | async-done | bytes 614416 | tf_op jit(solution)/shard_map/reduce_scatter | solution.py:312
  (264 shorter events, 121.4 us)
Async XLA Ops:
  8.0 84.3 %copy-start = (bf16[1280,1280]{1,0:T(8,128)(2,1)S(1)}, bf16[1280,1280]{1,0:T(8,128)(2,1)}, u32[]{:S(2)}) copy-start(bf16[1280,1280]{1,0:T(8,128)(2,1)} %param.20) | copy-start | bytes 9830404
  15.4 48.4 %copy-start.44 = (s32[3584]{0:T(1024)}, s32[3584]{0:T(1024)S(1)}, u32[]{:S(2)}) copy-start(s32[3584]{0:T(1024)S(1)} %eq.41) | copy-start | bytes 43012
  55.0 19.9 %copy-start.25 = (f32[512,64]{1,0:T(8,128)}, f32[512,64]{1,0:T(8,128)S(1)}, u32[]{:S(2)}) copy-start(f32[512,64]{1,0:T(8,128)S(1)} %get-tuple-element.102) | copy-start | bytes 393220
  97.5 21.9 %copy-start.71 = (pred[16,240]{1,0:T(8,128)(4,1)S(1)}, pred[16,240]{1,0:T(8,128)(4,1)}, u32[]{:S(2)}) copy-start(pred[16,240]{1,0:T(8,128)(4,1)} %broadcast_in_dim.145) | copy-start | bytes 11524
  119.5 228.4 %slice-start.3 = ((s8[9175040]{0:T(1024)(128)(4,1)}), s8[4194304]{0:T(1024)(128)(4,1)S(1)}, s32[]{:S(2)}) async-start(s8[9175040]{0:T(1024)(128)(4,1)} %bitcast.138), calls=%async_computation.20 | async-start | bytes 8388608
  119.5 228.4 %slice-start.4 = ((s8[9175040]{0:T(1024)(128)(4,1)}), s8[4194304]{0:T(1024)(128)(4,1)S(1)}, s32[]{:S(2)}) async-start(s8[9175040]{0:T(1024)(128)(4,1)} %bitcast.138), calls=%async_computation.21 | async-start | bytes 8388608
  126.5 221.4 %slice-start.5 = ((s8[9175040]{0:T(1024)(128)(4,1)}), s8[786432]{0:T(1024)(128)(4,1)S(1)}, s32[]{:S(2)}) async-start(s8[9175040]{0:T(1024)(128)(4,1)} %bitcast.138), calls=%async_computation.22 | async-start | bytes 1572864
  347.8 21.4 %copy-start.18 = (bf16[16,240,1280]{2,1,0:T(8,128)(2,1)}, bf16[16,240,1280]{2,1,0:T(8,128)(2,1)S(1)}, u32[]{:S(2)}) copy-start(bf16[16,240,1280]{2,1,0:T(8,128)(2,1)S(1)} %all_to_all.20) | copy-start | bytes 29491204
  405.0 220.2 %all-to-all-start.1 = ((bf16[16,240,1280]{2,1,0:T(8,128)(2,1)}), bf16[16,240,1280]{2,1,0:T(8,128)(2,1)}, u32[]{:S(2)}, u32[]{:S(2)}) async-start(bf16[16,240,1280]{2,1,0:T(8,128)(2,1)} %bitcast.119), calls=%async_computation.1 | async-start | bytes 19660800 | tf_op jit(solution)/shard_map/all_to_all | solution.py:214
  420.2 19.5 %copy-start.45 = (s32[3584]{0:T(1024)S(1)}, s32[3584]{0:T(1024)}, u32[]{:S(2)}) copy-start(s32[3584]{0:T(1024)} %copy-done.44) | copy-start | bytes 43012
  420.2 19.5 %copy-start.48 = (s32[3584]{0:T(1024)S(1)}, s32[3584]{0:T(1024)}, u32[]{:S(2)}) copy-start(s32[3584]{0:T(1024)} %copy-done.47) | copy-start | bytes 43012
  420.2 19.5 %copy-start.62 = (pred[3584]{0:T(1024)(128)(4,1)S(1)}, pred[3584]{0:T(1024)(128)(4,1)}, u32[]{:S(2)}) copy-start(pred[3584]{0:T(1024)(128)(4,1)} %and.62) | copy-start | bytes 10756
  420.2 19.5 %copy-start.50 = (s32[3840]{0:T(1024)S(1)}, s32[3840]{0:T(1024)}, u32[]{:S(2)}) copy-start(s32[3840]{0:T(1024)} %copy-done.49) | copy-start | bytes 46084
  420.2 20.2 %copy-start.40 = (bf16[1280,16]{0,1:T(8,128)(2,1)S(1)}, bf16[1280,16]{0,1:T(8,128)(2,1)}, u32[]{:S(2)}) copy-start(bf16[1280,16]{0,1:T(8,128)(2,1)} %param.22) | copy-start | bytes 122884
  439.7 209.7 %copy-start.60 = (pred[3584]{0:T(1024)(128)(4,1)}, pred[3584]{0:T(1024)(128)(4,1)S(1)}, u32[]{:S(2)}) copy-start(pred[3584]{0:T(1024)(128)(4,1)S(1)} %get-tuple-element.74) | copy-start | bytes 10756
  439.7 209.7 %copy-start.51 = (s32[4096]{0:T(1024)}, s32[4096]{0:T(1024)S(1)}, u32[]{:S(2)}) copy-start(s32[4096]{0:T(1024)S(1)} %pad_clamp_fusion.1) | copy-start | bytes 49156
  442.8 206.6 %copy-start.65 = (f32[512]{0:T(512)}, f32[512]{0:T(512)S(1)}, u32[]{:S(2)}) copy-start(f32[512]{0:T(512)S(1)} %fusion.74) | copy-start | bytes 6148
  649.4 12.5 copy-start.46
  664.2 11.7 copy-start.27
  676.0 25.4 %copy-start.70 = (pred[16,240]{1,0:T(8,128)(4,1)S(1)}, pred[16,240]{1,0:T(8,128)(4,1)}, u32[]{:S(2)}) copy-start(pred[16,240]{1,0:T(8,128)(4,1)} %broadcast_in_dim.150) | copy-start | bytes 11524
  710.9 222.6 %all-to-all-start.2 = ((bf16[16,240,1280]{2,1,0:T(8,128)(2,1)}), bf16[16,240,1280]{2,1,0:T(8,128)(2,1)}, u32[]{:S(2)}, u32[]{:S(2)}) async-start(bf16[16,240,1280]{2,1,0:T(8,128)(2,1)} %broadcast_select_fusion), calls=%async_computation.2 | async-start | bytes 19660800 | tf_op jit(solution)/shard_map/all_to_all | solution.py:245
  716.1 765.9 %all-reduce.7.cloned.1.call-start = ((), (), s32[]{:S(2)}) async-start(), calls=%async_computation.15 | async-start | bytes 163840
  719.2 764.2 %reduce-scatter.19.cloned.1.call-start = ((), (), s32[]{:S(2)}) async-start(), calls=%async_computation.14 | async-start | bytes 5734400 | tf_op jit(solution)/shard_map/reduce_scatter | solution.py:126
  948.5 645.4 %reduce-scatter.17.cloned.1.call-start = ((), (), s32[]{:S(2)}) async-start(), calls=%async_computation.13 | async-start | bytes 11468800 | tf_op jit(solution)/shard_map/reduce_scatter | solution.py:123
  1000.0 5.9 copy-start.64
  1000.0 598.0 %reduce-scatter.21.cloned.1.call-start = ((), (), s32[]{:S(2)}) async-start(), calls=%async_computation.16 | async-start | bytes 4730880
  1047.9 274.0 %all-to-all-start.3 = ((bf16[16,240,1280]{2,1,0:T(8,128)(2,1)}), bf16[16,240,1280]{2,1,0:T(8,128)(2,1)}, u32[]{:S(2)}, u32[]{:S(2)}) async-start(bf16[16,240,1280]{2,1,0:T(8,128)(2,1)} %bitcast.120), calls=%async_computation.3 | async-start | bytes 19660800 | tf_op jit(solution)/shard_map/all_to_all | solution.py:268
  1053.1 544.9 %reduce-scatter.15.cloned.1.call-start = ((), (), s32[]{:S(2)}) async-start(), calls=%async_computation.12 | async-start | bytes 9461760 | tf_op jit(solution)/shard_map/reduce_scatter | solution.py:316
  1061.5 260.5 %copy-start.52 = (s32[4096]{0:T(1024)S(1)}, s32[4096]{0:T(1024)}, u32[]{:S(2)}) copy-start(s32[4096]{0:T(1024)} %copy-done.51) | copy-start | bytes 49156
  1061.5 546.2 %reduce-scatter.13.cloned.1.call-start = ((), (), s32[]{:S(2)}) async-start(), calls=%async_computation.11 | async-start | bytes 6758400 | tf_op jit(solution)/shard_map/reduce_scatter | solution.py:313
  1321.9 24.2 %copy-start.61 = (pred[3584]{0:T(1024)(128)(4,1)S(1)}, pred[3584]{0:T(1024)(128)(4,1)}, u32[]{:S(2)}) copy-start(pred[3584]{0:T(1024)(128)(4,1)} %copy-done.60) | copy-start | bytes 10756
  1396.5 6.4 copy-start.3
  1396.5 6.4 copy-start.41
  1396.5 6.4 copy-start.43
  1396.5 6.4 copy-start.56
  1396.5 6.4 copy-start.68
  1411.4 411.6 %reduce-scatter.11.cloned.1.call-start = ((), (), s32[]{:S(2)}) async-start(), calls=%async_computation.10 | async-start | bytes 20275200 | tf_op jit(solution)/shard_map/reduce_scatter | solution.py:312
  1419.5 11.3 slice-start
  1419.5 11.3 slice-start.1
  1419.5 11.3 slice-start.2
  1430.8 6.4 copy-start.15
  1430.8 6.4 copy-start.17
  1448.7 6.3 copy-start.72
  1448.7 6.3 copy-start.73
  1539.9 19.9 %copy-start.28 = (f32[512,7]{1,0:T(8,128)S(1)}, f32[512,7]{1,0:T(8,128)}, u32[]{:S(2)}) copy-start(f32[512,7]{1,0:T(8,128)} %copy-done.27) | copy-start | bytes 43012
  1559.9 28.3 %copy-start.4 = (f32[512,1280]{1,0:T(8,128)S(1)}, f32[512,1280]{1,0:T(8,128)}, u32[]{:S(2)}) copy-start(f32[512,1280]{1,0:T(8,128)} %copy-done.2) | copy-start | bytes 7864324
  1559.9 28.3 %copy-start.32 = (bf16[512,896]{1,0:T(8,128)(2,1)S(1)}, bf16[512,896]{1,0:T(8,128)(2,1)}, u32[]{:S(2)}) copy-start(bf16[512,896]{1,0:T(8,128)(2,1)} %copy-done.31) | copy-start | bytes 2752516
  1559.9 28.3 %copy-start.76 = (bf16[896,1280]{1,0:T(8,128)(2,1)S(1)}, bf16[896,1280]{1,0:T(8,128)(2,1)}, u32[]{:S(2)}) copy-start(bf16[896,1280]{1,0:T(8,128)(2,1)} %param.24) | copy-start | bytes 6881284
  (45 other events, 131.0 us)
Sparse Core Ops, SparseCore 0:
  722.5 169.2 all-reduce.6
Sparse Core Ops, SparseCore 1:
  948.6 54.8 reduce-scatter.18
  1006.5 92.7 reduce-scatter.16
  1102.0 199.7 reduce-scatter.20
  1304.6 153.8 reduce-scatter.14
  1461.4 146.2 reduce-scatter.12
  1614.7 208.2 reduce-scatter.10
